TPU v7x, 32 devices: a whole 2x2x4 slice. The times are simulated.
32 devices in a mesh: groups: 2 (over y), samp: 4 (over z), feat: 4 (over x, core).
Axes of the slice: x: 2, y: 2, z: 4, core: 2. Of those that a mesh axis runs over, the one named last changes fastest.
Arguments:
- x_blocks: bfloat16 [64, 64, 128, 128], P(('groups', 'samp'), 'feat'), parts along dimension 0, may hold values from -6 to 6
- block_cols: int32 [64, 64], P('groups', 'feat'), parts along dimension 0, may hold values from 0 to 31
- labels: int32 [8192], P('groups'), parts along dimension 0, may hold values from 0 to 63
- group_ids: int32 [8192], P('groups'), parts along dimension 0, may hold values from 0 to 7, as said below
- picks: int32 [3, 32], P(None, 'groups'), parts along dimension 1, may hold values from 0 to 31, as said below
- w_init: float32 [16384, 64], P('feat'), may hold values from -2.253903 to 2.253903
Outputs:
- scores: float32 [8192, 64], P(('groups', 'samp')), parts along dimension 0
- adversary: float32 [16], P('groups'), parts along dimension 0
There are 2 independent parts, one for each index of `groups`. A program takes and returns all parts, laid end to end along the dimension named above; an argument that names none is the same for every part. Nothing has to cross between parts.
Inputs may be any that keep to these rules, and one draw needn't show every extreme that they name: `group_ids`: every row block of 128 samples holds every group at least once. `picks`: the entries of one step are distinct. Row block b is owned by index b // 8 of samp. The k-th aligned block of 4 entries of a step is the list of index k of samp; it names row blocks owned by index k or by the next index along samp (index 0 after the last); between one and 2 entries of each list name the next index's row blocks, exactly 2 in at least one list of every step.
All inputs are finite; a program needn't handle non-finite values.
Results may differ from a plain program's by a relative error of at most 0.00315.
The roundings to bfloat16 on the way count: a program that leaves them out, or rounds other values in their place, can miss the bound.
Values may be sent and summed in bfloat16 or wider, within the bound.
No kernel may reach another device: no remote copies, remote signals or barrier semaphores. Data moves between devices by JAX's collectives and lax.ppermute only.
A program may use at most 64 MiB of HBM per device.

v0:
```python
import jax
import jax.numpy as jnp
from jax import lax
from jax.sharding import PartitionSpec as P

GRP = 8
STEPS = 3
weight_rate = 8.0
adv_rate = 2.0


def per_device(x_blocks, block_cols, labels, group_ids, picks, w_init):
    row_blocks, per_row, block_size, _ = x_blocks.shape
    feat_rows, classes = w_init.shape
    col_blocks = feat_rows // block_size
    total_blocks = block_cols.shape[0]
    feat_count = lax.axis_size("feat")
    my_index = lax.axis_index("samp")
    step_rate = weight_rate * picks.shape[1] / (per_row * feat_count)
    class_range = jnp.arange(classes, dtype=jnp.int32)
    group_range = jnp.arange(GRP, dtype=jnp.int32)
    block_range = jnp.arange(total_blocks, dtype=jnp.int32)
    col_range = jnp.arange(col_blocks, dtype=jnp.int32)
    sample_groups = (group_ids[:, None] == group_range[None, :]).astype(jnp.float32)
    block_groups = jnp.sum(sample_groups.reshape(total_blocks, block_size, GRP), axis=1)
    own_start = my_index * row_blocks
    own_cols = lax.dynamic_slice_in_dim(block_cols, own_start, row_blocks, 0)
    own_labels = lax.dynamic_slice_in_dim(
        labels, own_start * block_size, row_blocks * block_size, 0
    )
    own_groups = lax.dynamic_slice_in_dim(
        group_ids, own_start * block_size, row_blocks * block_size, 0
    )

    def total_logits(x_rows, col_rows, weights_bf):
        tiles = weights_bf.reshape(col_blocks, block_size, classes)[col_rows]
        partial_sum = jnp.einsum(
            "rbij,rbjc->ric", x_rows, tiles, preferred_element_type=jnp.float32
        )
        summed = lax.psum(partial_sum, "feat")
        return summed.reshape(-1, classes)

    def evaluate(row_data, weights_bf, adversary, counts):
        x_rows, col_rows, label_rows, group_rows, mult_rows = row_data
        logits = total_logits(x_rows, col_rows, weights_bf)
        label_hot = (label_rows[:, None] == class_range[None, :]).astype(jnp.float32)
        group_hot = (group_rows[:, None] == group_range[None, :]).astype(jnp.float32)
        log_total = jax.nn.logsumexp(logits, axis=-1)
        cross = log_total - jnp.sum(logits * label_hot, axis=-1)
        probs = jnp.exp(logits - log_total[:, None])
        local_loss = jnp.dot(mult_rows * cross, group_hot, precision=lax.Precision.HIGHEST)
        loss = lax.psum(local_loss, "samp") / counts
        coef = jnp.dot(group_hot, adversary / counts, precision=lax.Precision.HIGHEST) * mult_rows
        dz_rows = (coef[:, None] * (probs - label_hot)).astype(jnp.bfloat16)
        blocks_here = x_rows.shape[0]
        dz_blocks = dz_rows.reshape(blocks_here, block_size, classes)
        grad_tiles = jnp.einsum(
            "rbij,ric->rbjc", x_rows, dz_blocks, preferred_element_type=jnp.float32
        )
        grad_tiles = grad_tiles.reshape(blocks_here * per_row, block_size * classes)
        col_hot = (col_rows.reshape(-1)[:, None] == col_range[None, :]).astype(jnp.float32)
        grad_local = jnp.dot(col_hot.T, grad_tiles, precision=lax.Precision.HIGHEST)
        return (loss, grad_local.reshape(feat_rows, classes))

    def advance(state, grad_local):
        grad_total = lax.psum(grad_local, "samp")
        new_state = state - step_rate * grad_total
        return (new_state, new_state.astype(jnp.bfloat16))

    state = w_init
    weights_bf = w_init.astype(jnp.bfloat16)
    adversary = jnp.full((GRP,), 1.0 / GRP, jnp.float32)
    for step in range(STEPS):
        block_hits = jnp.sum(
            (picks[step][:, None] == block_range[None, :]).astype(jnp.float32), axis=0
        )
        counts = jnp.dot(block_hits, block_groups, precision=lax.Precision.HIGHEST)
        own_hits = lax.dynamic_slice_in_dim(block_hits, own_start, row_blocks, 0)
        row_data = (x_blocks, own_cols, own_labels, own_groups, jnp.repeat(own_hits, block_size))
        loss_first, grad_first = evaluate(row_data, weights_bf, adversary, counts)
        half_state, half_bf = advance(state, grad_first)
        half_adv = jax.nn.softmax(jnp.log(adversary) + adv_rate * loss_first)
        loss_second, grad_second = evaluate(row_data, half_bf, half_adv, counts)
        state, weights_bf = advance(state, grad_second)
        adversary = jax.nn.softmax(jnp.log(adversary) + adv_rate * loss_second)
    return (total_logits(x_blocks, own_cols, weights_bf), adversary)


def solution(mesh):
    in_specs = (
        P(("groups", "samp"), "feat", None, None),
        P("groups", "feat"),
        P("groups"),
        P("groups"),
        P(None, "groups"),
        P("feat", None),
    )
    out_specs = (P(("groups", "samp"), None), P("groups"))
    return jax.shard_map(
        per_device, mesh=mesh, in_specs=in_specs, out_specs=out_specs, check_vma=False
    )
```

profile of v0, /device:TPU:0, one launch (start us, length us, event | category | flops | bytes accessed | tf_op | source)
XLA Modules:
  0.0 842.0 jit_solution(14522523979013200713)
XLA Ops:
  10.5 4.4 convolution_bitcast_fusion.12
  16.2 33.7 %all-reduce.17.cloned.1.call-done = f32[8,128,64]{1,2,0:T(8,128)} async-done(((f32[8,128,64]{1,2,0:T(8,128)}), f32[8,128,64]{1,2,0:T(8,128)}) %all-reduce.17.cloned.1.call-update) | async-done | bytes 262160 | tf_op jit(solution)/shard_map/psum | solution.py:40
  51.9 5.0 convolution_bitcast_fusion.5
  56.8 6.9 copy.85
  63.7 7.9 reshape.440
  71.6 3.8 fusion.69
  80.9 51.9 %all-reduce.19.cloned.1.call-done = f32[4096,64]{0,1:T(8,128)} async-done(((f32[4096,64]{0,1:T(8,128)}), f32[4096,64]{0,1:T(8,128)}) %all-reduce.19.cloned.1.call-update) | async-done | bytes 1048592 | tf_op jit(solution)/shard_map/psum | solution.py:66
  136.4 5.1 convolution_bitcast_fusion.11
  141.5 31.5 %all-reduce.21.cloned.1.call-done = f32[8,128,64]{1,2,0:T(8,128)} async-done(((f32[8,128,64]{1,2,0:T(8,128)}), f32[8,128,64]{1,2,0:T(8,128)}) %all-reduce.21.cloned.1.call-update) | async-done | bytes 262160 | tf_op jit(solution)/shard_map/psum | solution.py:40
  175.8 12.2 %all-reduce.2 = (f32[8]{0:T(128)S(1)}, f32[8]{0:T(128)S(1)}) all-reduce(f32[8]{0:T(128)S(1)} %convolution_bitcast_fusion.21, f32[8]{0:T(128)S(1)} %convolution_bitcast_fusion.20), channel_id=1, replica_groups=mesh['groups'=2,'samp'=4,'feat'=4] {'samp'}, use_global_device_ids=true, to_apply=%region_5.0 | all-reduce | flops 16 | bytes 128 | tf_op jit(solution)/shard_map/psum | solution.py:52
  192.4 5.0 convolution_bitcast_fusion.4
  197.3 6.9 copy.88
  204.2 7.9 reshape.443
  212.1 3.8 fusion.68
  223.3 47.3 %all-reduce.23.cloned.1.call-done = f32[4096,64]{0,1:T(8,128)} async-done(((f32[4096,64]{0,1:T(8,128)}), f32[4096,64]{0,1:T(8,128)}) %all-reduce.23.cloned.1.call-update) | async-done | bytes 1048592 | tf_op jit(solution)/shard_map/psum | solution.py:66
  274.1 5.1 convolution_bitcast_fusion.10
  279.3 31.4 %all-reduce.25.cloned.1.call-done = f32[8,128,64]{1,2,0:T(8,128)} async-done(((f32[8,128,64]{1,2,0:T(8,128)}), f32[8,128,64]{1,2,0:T(8,128)}) %all-reduce.25.cloned.1.call-update) | async-done | bytes 262160 | tf_op jit(solution)/shard_map/psum | solution.py:40
  312.8 5.0 convolution_bitcast_fusion.3
  317.7 6.9 copy.91
  324.6 7.9 reshape.447
  332.5 4.8 fusion.67
  337.3 3.2 reshape.448
  344.0 51.8 %all-reduce.27.cloned.1.call-done = f32[4096,64]{0,1:T(8,128)} async-done(((f32[4096,64]{0,1:T(8,128)}), f32[4096,64]{0,1:T(8,128)}) %all-reduce.27.cloned.1.call-update) | async-done | bytes 1048592 | tf_op jit(solution)/shard_map/psum | solution.py:66
  399.3 5.1 convolution_bitcast_fusion.9
  404.4 31.4 %all-reduce.29.cloned.1.call-done = f32[8,128,64]{1,2,0:T(8,128)} async-done(((f32[8,128,64]{1,2,0:T(8,128)}), f32[8,128,64]{1,2,0:T(8,128)}) %all-reduce.29.cloned.1.call-update) | async-done | bytes 262160 | tf_op jit(solution)/shard_map/psum | solution.py:40
  438.7 11.7 %all-reduce.1 = (f32[8]{0:T(128)S(1)}, f32[8]{0:T(128)S(1)}) all-reduce(f32[8]{0:T(128)S(1)} %convolution_bitcast_fusion.19, f32[8]{0:T(128)S(1)} %convolution_bitcast_fusion.18), channel_id=1, replica_groups=mesh['groups'=2,'samp'=4,'feat'=4] {'samp'}, use_global_device_ids=true, to_apply=%region_23.0 | all-reduce | flops 16 | bytes 128 | tf_op jit(solution)/shard_map/psum | solution.py:52
  455.9 5.0 convolution_bitcast_fusion.2
  460.9 6.9 copy.94
  467.8 7.9 reshape.450
  475.7 4.8 fusion.66
  490.0 46.1 %all-reduce.31.cloned.1.call-done = f32[4096,64]{0,1:T(8,128)} async-done(((f32[4096,64]{0,1:T(8,128)}), f32[4096,64]{0,1:T(8,128)}) %all-reduce.31.cloned.1.call-update) | async-done | bytes 1048592 | tf_op jit(solution)/shard_map/psum | solution.py:66
  539.6 4.4 convolution_bitcast_fusion.8
  544.4 31.2 %all-reduce.33.cloned.1.call-done = f32[8,128,64]{1,2,0:T(8,128)} async-done(((f32[8,128,64]{1,2,0:T(8,128)}), f32[8,128,64]{1,2,0:T(8,128)}) %all-reduce.33.cloned.1.call-update) | async-done | bytes 262160 | tf_op jit(solution)/shard_map/psum | solution.py:40
  577.7 5.0 convolution_bitcast_fusion.1
  582.7 6.9 copy.97
  589.6 7.9 reshape.454
  597.5 3.8 fusion.65
  606.7 51.9 %all-reduce.35.cloned.1.call-done = f32[4096,64]{0,1:T(8,128)} async-done(((f32[4096,64]{0,1:T(8,128)}), f32[4096,64]{0,1:T(8,128)}) %all-reduce.35.cloned.1.call-update) | async-done | bytes 1048592 | tf_op jit(solution)/shard_map/psum | solution.py:66
  661.0 4.4 convolution_bitcast_fusion.7
  665.5 31.5 %all-reduce.37.cloned.1.call-done = f32[8,128,64]{1,2,0:T(8,128)} async-done(((f32[8,128,64]{1,2,0:T(8,128)}), f32[8,128,64]{1,2,0:T(8,128)}) %all-reduce.37.cloned.1.call-update) | async-done | bytes 262160 | tf_op jit(solution)/shard_map/psum | solution.py:40
  699.8 11.7 %all-reduce = (f32[8]{0:T(128)S(1)}, f32[8]{0:T(128)S(1)}) all-reduce(f32[8]{0:T(128)S(1)} %convolution_bitcast_fusion.17, f32[8]{0:T(128)S(1)} %convolution_bitcast_fusion.16), channel_id=1, replica_groups=mesh['groups'=2,'samp'=4,'feat'=4] {'samp'}, use_global_device_ids=true, to_apply=%region_40.0 | all-reduce | flops 16 | bytes 128 | tf_op jit(solution)/shard_map/psum | solution.py:52
  717.0 5.0 convolution_bitcast_fusion
  722.0 6.9 copy.100
  728.9 7.9 reshape.457
  736.8 3.8 fusion.64
  747.3 47.9 %all-reduce.39.cloned.1.call-done = f32[4096,64]{0,1:T(8,128)} async-done(((f32[4096,64]{0,1:T(8,128)}), f32[4096,64]{0,1:T(8,128)}) %all-reduce.39.cloned.1.call-update) | async-done | bytes 1048592 | tf_op jit(solution)/shard_map/psum | solution.py:66
  797.6 3.7 convolution_bitcast_fusion.6
  803.8 29.7 %all-reduce.41.cloned.1.call-done = f32[1024,64]{0,1:T(8,128)} async-done(((f32[1024,64]{0,1:T(8,128)}), f32[1024,64]{0,1:T(8,128)}) %all-reduce.41.cloned.1.call-update) | async-done | bytes 262160 | tf_op jit(solution)/shard_map/psum | solution.py:40
  (145 shorter events, 95.8 us)
Async XLA Ops:
  7.2 9.0 %copy-start = (s32[4096]{0:T(1024)S(1)}, s32[4096]{0:T(1024)}, u32[]{:S(2)}) copy-start(s32[4096]{0:T(1024)} %param.8) | copy-start | bytes 49156
  7.2 42.6 %all-reduce.17.cloned.1.call-start = ((), (), s32[]{:S(2)}) async-start(), calls=%async_computation | async-start | bytes 524288 | tf_op jit(solution)/shard_map/psum | solution.py:40
  10.5 4.5 copy-start.7
  10.5 4.7 copy-start.6
  15.0 117.8 %all-reduce.19.cloned.1.call-start = ((), (), s32[]{:S(2)}) async-start(), calls=%async_computation.1 | async-start | bytes 2097152 | tf_op jit(solution)/shard_map/psum | solution.py:66
  75.4 57.4 %copy-start.2 = (f32[4096,64]{0,1:T(8,128)S(1)}, f32[4096,64]{0,1:T(8,128)}, u32[]{:S(2)}) copy-start(f32[4096,64]{0,1:T(8,128)} %param.11) | copy-start | bytes 3145732
  80.8 92.1 %all-reduce.21.cloned.1.call-start = ((), (), s32[]{:S(2)}) async-start(), calls=%async_computation.2 | async-start | bytes 524288 | tf_op jit(solution)/shard_map/psum | solution.py:40
  141.4 129.2 %all-reduce.23.cloned.1.call-start = ((), (), s32[]{:S(2)}) async-start(), calls=%async_computation.3 | async-start | bytes 2097152 | tf_op jit(solution)/shard_map/psum | solution.py:66
  221.3 89.4 %all-reduce.25.cloned.1.call-start = ((), (), s32[]{:S(2)}) async-start(), calls=%async_computation.4 | async-start | bytes 524288 | tf_op jit(solution)/shard_map/psum | solution.py:40
  279.2 116.5 %all-reduce.27.cloned.1.call-start = ((), (), s32[]{:S(2)}) async-start(), calls=%async_computation.5 | async-start | bytes 2097152 | tf_op jit(solution)/shard_map/psum | solution.py:66
  337.3 58.4 %copy-start.3 = (f32[4096,64]{0,1:T(8,128)S(1)}, f32[4096,64]{0,1:T(8,128)}, u32[]{:S(2)}) copy-start(f32[4096,64]{0,1:T(8,128)} %all-reduce.23.cloned.1.call-done) | copy-start | bytes 3145732
  343.7 92.1 %all-reduce.29.cloned.1.call-start = ((), (), s32[]{:S(2)}) async-start(), calls=%async_computation.6 | async-start | bytes 524288 | tf_op jit(solution)/shard_map/psum | solution.py:40
  404.4 131.7 %all-reduce.31.cloned.1.call-start = ((), (), s32[]{:S(2)}) async-start(), calls=%async_computation.7 | async-start | bytes 2097152 | tf_op jit(solution)/shard_map/psum | solution.py:66
  486.8 88.9 %all-reduce.33.cloned.1.call-start = ((), (), s32[]{:S(2)}) async-start(), calls=%async_computation.8 | async-start | bytes 524288 | tf_op jit(solution)/shard_map/psum | solution.py:40
  544.1 114.6 %all-reduce.35.cloned.1.call-start = ((), (), s32[]{:S(2)}) async-start(), calls=%async_computation.9 | async-start | bytes 2097152 | tf_op jit(solution)/shard_map/psum | solution.py:66
  601.3 57.4 %copy-start.4 = (f32[4096,64]{0,1:T(8,128)S(1)}, f32[4096,64]{0,1:T(8,128)}, u32[]{:S(2)}) copy-start(f32[4096,64]{0,1:T(8,128)} %get-tuple-element.29) | copy-start | bytes 3145732
  606.7 90.3 %all-reduce.37.cloned.1.call-start = ((), (), s32[]{:S(2)}) async-start(), calls=%async_computation.10 | async-start | bytes 524288 | tf_op jit(solution)/shard_map/psum | solution.py:40
  665.4 129.8 %all-reduce.39.cloned.1.call-start = ((), (), s32[]{:S(2)}) async-start(), calls=%async_computation.11 | async-start | bytes 2097152 | tf_op jit(solution)/shard_map/psum | solution.py:66
  740.6 54.6 %copy-start.5 = (f32[4096,64]{0,1:T(8,128)S(1)}, f32[4096,64]{0,1:T(8,128)}, u32[]{:S(2)}) copy-start(f32[4096,64]{0,1:T(8,128)} %get-tuple-element.29) | copy-start | bytes 3145732
  746.0 87.6 %all-reduce.41.cloned.1.call-start = ((), (), s32[]{:S(2)}) async-start(), calls=%async_computation.12 | async-start | bytes 524288 | tf_op jit(solution)/shard_map/psum | solution.py:40
  796.6 38.6 %copy-start.1 = (s32[4096]{0:T(1024)S(1)}, s32[4096]{0:T(1024)}, u32[]{:S(2)}) copy-start(s32[4096]{0:T(1024)} %param.8) | copy-start | bytes 49156
Sparse Core Ops, SparseCore 0:
  15.1 34.6 all-reduce.16
  80.9 51.8 all-reduce.18
  141.6 31.3 all-reduce.20
  221.4 49.1 all-reduce.22
  279.3 31.3 all-reduce.24
  343.9 51.8 all-reduce.26
  404.5 31.3 all-reduce.28
  486.9 49.1 all-reduce.30
  544.2 31.4 all-reduce.32
  606.8 51.8 all-reduce.34
  665.5 31.3 all-reduce.36
  746.1 49.0 all-reduce.38
  802.2 31.3 all-reduce.40
where the time goes:
time: 851 us; the launch traced here: 842 us
  waiting for transfers between devices  518 us (61%)
  local copies, waits for them, and re-layouts  136 us (16%)
  matrix products  98.5 us (12%)
  other arithmetic  38.8 us (5%)
  blocking collectives  35.5 us (4%)
  between operations  14.6 us (2%)
    psum x6, waiting for transfers between devices, advance(): grad_total = lax.psum(grad_local, 'samp')  297 us
    psum x7, waiting for transfers between devices, total_logits(): summed = lax.psum(partial_sum, 'feat')  220 us
    reshape x6, local copies, waits for them, and re-layouts, evaluate(): grad_tiles = grad_tiles.reshape(blocks_here * per_row, block_size * classes)  47.3 us
    dot_general x6, local copies, waits for them, and re-layouts, evaluate(): jnp.einsum('rbij,ric->rbjc', x_rows, dz_blocks, preferred_element_type=jn...  41.4 us
    psum x3, blocking collectives, evaluate(): loss = lax.psum(local_loss, 'samp') / counts  35.5 us
    reshape x12, local copies, waits for them, and re-layouts, evaluate(): return (loss, grad_local.reshape(feat_rows, classes))  34.1 us
    dot_general x7, matrix products, total_logits(): jnp.einsum('rbij,rbjc->ric', x_rows, tiles, preferred_element_type=jnp.fl...  32.2 us
    dot_general x6, matrix products, evaluate(): jnp.einsum('rbij,ric->rbjc', x_rows, dz_blocks, preferred_element_type=jn...  29.8 us
  transfers between devices with their start and end apart: 13, of which 13 were waited for; matrix products, arithmetic and copies ran while one was open for 1% of the time, Pallas kernels for 0%

commit v1 on v0

--- a/solution.py
+++ b/solution.py
@@ -37,7 +37,9 @@
         partial_sum = jnp.einsum(
             "rbij,rbjc->ric", x_rows, tiles, preferred_element_type=jnp.float32
         )
-        summed = lax.psum(partial_sum, "feat")
+        summed = partial_sum
+        for hop in (1, 2):
+            summed = summed + lax.ppermute(summed, "feat", [(dev, dev ^ hop) for dev in range(4)])
         return summed.reshape(-1, classes)
 
     def evaluate(row_data, weights_bf, adversary, counts):

time: 851 us -> 676 us (0.79)
  waiting for transfers between devices: 518 us -> 355 us
  starting transfers between devices: 0.92 us -> 14 us
  other arithmetic: 38.8 us -> 28.6 us
  matrix products: 98.5 us -> 89.8 us
    psum x7 -> x0, waiting for transfers between devices: 220 us -> none  [total_logits(): summed = lax.psum(partial_sum, 'feat')]
    ppermute x0 -> x14, waiting for transfers between devices: none -> 49 us  [total_logits(): lax.ppermute(summed, 'feat', [(dev, dev ^ hop) for dev in range(4)])]
    ppermute x0 -> x14, starting transfers between devices: none -> 13.3 us  [total_logits(): lax.ppermute(summed, 'feat', [(dev, dev ^ hop) for dev in range(4)])]
    psum x6, waiting for transfers between devices: 297 us -> 306 us  [advance(): grad_total = lax.psum(grad_local, 'samp')]
  transfers between devices with their start and end apart: 13 -> 20, of which waited for: 13 -> 19; matrix products, arithmetic and copies ran while one was open for 1% -> 1% of each run, Pallas kernels for 0% -> 0%
where the time goes in v1:
time: 676 us; the launch traced here: 667 us
  waiting for transfers between devices  355 us (53%)
  local copies, waits for them, and re-layouts  134 us (20%)
  matrix products  89.8 us (13%)
  blocking collectives  31 us (5%)
  other arithmetic  28.6 us (4%)
  between operations  15.1 us (2%)
  starting transfers between devices  14 us (2%)
    psum x6, waiting for transfers between devices, advance(): grad_total = lax.psum(grad_local, 'samp')  306 us
    ppermute x14, waiting for transfers between devices, total_logits(): lax.ppermute(summed, 'feat', [(dev, dev ^ hop) for dev in range(4)])  49 us
    reshape x6, local copies, waits for them, and re-layouts, evaluate(): grad_tiles = grad_tiles.reshape(blocks_here * per_row, block_size * classes)  47.3 us
    dot_general x6, local copies, waits for them, and re-layouts, evaluate(): jnp.einsum('rbij,ric->rbjc', x_rows, dz_blocks, preferred_element_type=jn...  41.4 us
    reshape x12, local copies, waits for them, and re-layouts, evaluate(): return (loss, grad_local.reshape(feat_rows, classes))  34.1 us
    psum x3, blocking collectives, evaluate(): loss = lax.psum(local_loss, 'samp') / counts  31 us
    dot_general x7, matrix products, total_logits(): jnp.einsum('rbij,rbjc->ric', x_rows, tiles, preferred_element_type=jnp.fl...  28.2 us
    dot_general x6, matrix products, evaluate(): jnp.einsum('rbij,ric->rbjc', x_rows, dz_blocks, preferred_element_type=jn...  24.9 us
  transfers between devices with their start and end apart: 20, of which 19 were waited for; matrix products, arithmetic and copies ran while one was open for 1% of the time, Pallas kernels for 0%

profile of v1, /device:TPU:0, one launch (start us, length us, event | category | flops | bytes accessed | tf_op | source)
XLA Modules:
  0.0 667.2 jit_solution(16535051827249323139)
XLA Ops:
  10.5 3.7 convolution_bitcast_fusion.12
  19.2 6.3 collective-permute-done.1
  25.6 4.9 convolution_bitcast_fusion.5
  30.5 6.9 %copy.85 = f32[8,16,128,64]{3,2,1,0:T(8,128)} copy(f32[8,16,128,64]{2,3,1,0:T(8,128)} %convolution_bitcast_fusion.5) | data formatting | bytes 8388608 | tf_op jit(solution)/shard_map/rbij,ric->rbjc/dot_general | solution.py:59
  37.4 7.9 %reshape.440 = f32[128,8192]{1,0:T(8,128)} reshape(f32[8,16,128,64]{3,2,1,0:T(8,128)} %copy.85) | data formatting | bytes 8388608 | tf_op jit(solution)/shard_map/reshape | solution.py:62
  45.3 3.8 fusion.69
  51.3 3.2 copy.86
  54.6 53.4 %all-reduce.10.cloned.1.call-done = f32[4096,64]{0,1:T(8,128)} async-done(((f32[4096,64]{0,1:T(8,128)}), f32[4096,64]{0,1:T(8,128)}) %all-reduce.10.cloned.1.call-update) | async-done | bytes 1048592 | tf_op jit(solution)/shard_map/psum | solution.py:68
  111.5 4.3 convolution_bitcast_fusion.11
  119.1 6.9 %collective-permute-done.3 = f32[8,128,64]{1,2,0:T(8,128)S(1)} collective-permute-done((f32[8,128,64]{1,2,0:T(8,128)S(1)}, f32[8,128,64]{1,2,0:T(8,128)S(1)}, u32[]{:S(2)}, u32[]{:S(2)}) %collective-permute-start.3) | collective-permute-done | bytes 262176 | tf_op jit(solution)/shard_map/ppermute | solution.py:42
  127.0 10.3 %all-reduce.2 = (f32[8]{0:T(128)S(1)}, f32[8]{0:T(128)S(1)}) all-reduce(f32[8]{0:T(128)S(1)} %convolution_bitcast_fusion.21, f32[8]{0:T(128)S(1)} %convolution_bitcast_fusion.20), channel_id=1, replica_groups=mesh['groups'=2,'samp'=4,'feat'=4] {'samp'}, use_global_device_ids=true, to_apply=%region_4.0 | all-reduce | flops 16 | bytes 128 | tf_op jit(solution)/shard_map/psum | solution.py:54
  141.7 4.9 convolution_bitcast_fusion.4
  146.6 6.9 %copy.88 = f32[8,16,128,64]{3,2,1,0:T(8,128)} copy(f32[8,16,128,64]{2,3,1,0:T(8,128)} %convolution_bitcast_fusion.4) | data formatting | bytes 8388608 | tf_op jit(solution)/shard_map/rbij,ric->rbjc/dot_general | solution.py:59
  153.5 7.9 %reshape.443 = f32[128,8192]{1,0:T(8,128)} reshape(f32[8,16,128,64]{3,2,1,0:T(8,128)} %copy.88) | data formatting | bytes 8388608 | tf_op jit(solution)/shard_map/reshape | solution.py:62
  161.4 3.8 fusion.68
  170.7 50.0 %all-reduce.12.cloned.1.call-done = f32[4096,64]{0,1:T(8,128)} async-done(((f32[4096,64]{0,1:T(8,128)}), f32[4096,64]{0,1:T(8,128)}) %all-reduce.12.cloned.1.call-update) | async-done | bytes 1048592 | tf_op jit(solution)/shard_map/psum | solution.py:68
  224.2 4.5 convolution_bitcast_fusion.10
  233.6 5.1 collective-permute-done.5
  241.6 6.9 %copy.91 = f32[8,16,128,64]{3,2,1,0:T(8,128)} copy(f32[8,16,128,64]{2,3,1,0:T(8,128)} %convolution_bitcast_fusion.3) | data formatting | bytes 8388608 | tf_op jit(solution)/shard_map/rbij,ric->rbjc/dot_general | solution.py:59
  248.5 7.9 %reshape.447 = f32[128,8192]{1,0:T(8,128)} reshape(f32[8,16,128,64]{3,2,1,0:T(8,128)} %copy.91) | data formatting | bytes 8388608 | tf_op jit(solution)/shard_map/reshape | solution.py:62
  256.4 4.8 fusion.67
  261.2 3.2 reshape.448
  264.5 3.2 copy.92
  267.9 51.1 %all-reduce.14.cloned.1.call-done = f32[4096,64]{0,1:T(8,128)} async-done(((f32[4096,64]{0,1:T(8,128)}), f32[4096,64]{0,1:T(8,128)}) %all-reduce.14.cloned.1.call-update) | async-done | bytes 1048592 | tf_op jit(solution)/shard_map/psum | solution.py:68
  322.6 4.3 convolution_bitcast_fusion.9
  330.1 6.9 %collective-permute-done.7 = f32[8,128,64]{1,2,0:T(8,128)S(1)} collective-permute-done((f32[8,128,64]{1,2,0:T(8,128)S(1)}, f32[8,128,64]{1,2,0:T(8,128)S(1)}, u32[]{:S(2)}, u32[]{:S(2)}) %collective-permute-start.7) | collective-permute-done | bytes 262176 | tf_op jit(solution)/shard_map/ppermute | solution.py:42
  338.0 10.2 %all-reduce.1 = (f32[8]{0:T(128)S(1)}, f32[8]{0:T(128)S(1)}) all-reduce(f32[8]{0:T(128)S(1)} %convolution_bitcast_fusion.19, f32[8]{0:T(128)S(1)} %convolution_bitcast_fusion.18), channel_id=1, replica_groups=mesh['groups'=2,'samp'=4,'feat'=4] {'samp'}, use_global_device_ids=true, to_apply=%region_20.0 | all-reduce | flops 16 | bytes 128 | tf_op jit(solution)/shard_map/psum | solution.py:54
  353.8 4.9 convolution_bitcast_fusion.2
  358.7 6.9 %copy.94 = f32[8,16,128,64]{3,2,1,0:T(8,128)} copy(f32[8,16,128,64]{2,3,1,0:T(8,128)} %convolution_bitcast_fusion.2) | data formatting | bytes 8388608 | tf_op jit(solution)/shard_map/rbij,ric->rbjc/dot_general | solution.py:59
  365.6 7.9 %reshape.450 = f32[128,8192]{1,0:T(8,128)} reshape(f32[8,16,128,64]{3,2,1,0:T(8,128)} %copy.94) | data formatting | bytes 8388608 | tf_op jit(solution)/shard_map/reshape | solution.py:62
  373.5 4.8 fusion.66
  384.9 49.8 %all-reduce.16.cloned.1.call-done = f32[4096,64]{0,1:T(8,128)} async-done(((f32[4096,64]{0,1:T(8,128)}), f32[4096,64]{0,1:T(8,128)}) %all-reduce.16.cloned.1.call-update) | async-done | bytes 1048592 | tf_op jit(solution)/shard_map/psum | solution.py:68
  438.3 3.9 convolution_bitcast_fusion.8
  447.2 5.4 collective-permute-done.9
  455.4 6.9 %copy.97 = f32[8,16,128,64]{3,2,1,0:T(8,128)} copy(f32[8,16,128,64]{2,3,1,0:T(8,128)} %convolution_bitcast_fusion.1) | data formatting | bytes 8388608 | tf_op jit(solution)/shard_map/rbij,ric->rbjc/dot_general | solution.py:59
  462.3 7.9 %reshape.454 = f32[128,8192]{1,0:T(8,128)} reshape(f32[8,16,128,64]{3,2,1,0:T(8,128)} %copy.97) | data formatting | bytes 8388608 | tf_op jit(solution)/shard_map/reshape | solution.py:62
  470.2 3.8 fusion.65
  479.5 51.3 %all-reduce.18.cloned.1.call-done = f32[4096,64]{0,1:T(8,128)} async-done(((f32[4096,64]{0,1:T(8,128)}), f32[4096,64]{0,1:T(8,128)}) %all-reduce.18.cloned.1.call-update) | async-done | bytes 1048592 | tf_op jit(solution)/shard_map/psum | solution.py:68
  533.1 3.7 convolution_bitcast_fusion.7
  540.0 6.9 %collective-permute-done.11 = f32[8,128,64]{1,2,0:T(8,128)S(1)} collective-permute-done((f32[8,128,64]{1,2,0:T(8,128)S(1)}, f32[8,128,64]{1,2,0:T(8,128)S(1)}, u32[]{:S(2)}, u32[]{:S(2)}) %collective-permute-start.11) | collective-permute-done | bytes 262176 | tf_op jit(solution)/shard_map/ppermute | solution.py:42
  547.9 10.5 %all-reduce = (f32[8]{0:T(128)S(1)}, f32[8]{0:T(128)S(1)}) all-reduce(f32[8]{0:T(128)S(1)} %convolution_bitcast_fusion.17, f32[8]{0:T(128)S(1)} %convolution_bitcast_fusion.16), channel_id=1, replica_groups=mesh['groups'=2,'samp'=4,'feat'=4] {'samp'}, use_global_device_ids=true, to_apply=%region_35.0 | all-reduce | flops 16 | bytes 128 | tf_op jit(solution)/shard_map/psum | solution.py:54
  564.0 4.9 convolution_bitcast_fusion
  568.8 6.9 %copy.100 = f32[8,16,128,64]{3,2,1,0:T(8,128)} copy(f32[8,16,128,64]{2,3,1,0:T(8,128)} %convolution_bitcast_fusion) | data formatting | bytes 8388608 | tf_op jit(solution)/shard_map/rbij,ric->rbjc/dot_general | solution.py:59
  575.8 7.9 %reshape.457 = f32[128,8192]{1,0:T(8,128)} reshape(f32[8,16,128,64]{3,2,1,0:T(8,128)} %copy.100) | data formatting | bytes 8388608 | tf_op jit(solution)/shard_map/reshape | solution.py:62
  583.6 3.8 fusion.64
  592.8 50.1 %all-reduce.20.cloned.1.call-done = f32[4096,64]{0,1:T(8,128)} async-done(((f32[4096,64]{0,1:T(8,128)}), f32[4096,64]{0,1:T(8,128)}) %all-reduce.20.cloned.1.call-update) | async-done | bytes 1048592 | tf_op jit(solution)/shard_map/psum | solution.py:68
  645.3 3.7 convolution_bitcast_fusion.6
  655.1 4.0 collective-permute-done.13
  (162 shorter events, 103.0 us)
Async XLA Ops:
  7.2 11.7 %copy-start = (s32[4096]{0:T(1024)S(1)}, s32[4096]{0:T(1024)}, u32[]{:S(2)}) copy-start(s32[4096]{0:T(1024)} %param.8) | copy-start | bytes 49156
  7.2 100.8 %all-reduce.10.cloned.1.call-start = ((), (), s32[]{:S(2)}) async-start(), calls=%async_computation | async-start | bytes 2097152 | tf_op jit(solution)/shard_map/psum | solution.py:68
  10.5 4.3 copy-start.9
  10.5 4.4 copy-start.8
  14.2 1.7 collective-permute-start
  16.0 9.5 %collective-permute-start.1 = (f32[8,128,64]{1,2,0:T(8,128)S(1)}, f32[8,128,64]{1,2,0:T(8,128)S(1)}, u32[]{:S(2)}, u32[]{:S(2)}) collective-permute-start(f32[8,128,64]{1,2,0:T(8,128)S(1)} %add.154), channel_id=1, source_target_pairs={{0,2},{1,3},{2,0},{3,1},{4,6},{5,7},{6,4},{7,5},{8,10},{9,11},{10,... | collective-permute-start | bytes 786440 | tf_op jit(solution)/shard_map/ppermute | solution.py:42
  49.1 58.9 %copy-start.4 = (f32[4096,64]{0,1:T(8,128)S(1)}, f32[4096,64]{0,1:T(8,128)}, u32[]{:S(2)}) copy-start(f32[4096,64]{0,1:T(8,128)} %param.11) | copy-start | bytes 3145732
  54.5 166.2 %all-reduce.12.cloned.1.call-start = ((), (), s32[]{:S(2)}) async-start(), calls=%async_computation.1 | async-start | bytes 2097152 | tf_op jit(solution)/shard_map/psum | solution.py:68
  115.9 1.6 collective-permute-start.2
  117.5 8.4 %collective-permute-start.3 = (f32[8,128,64]{1,2,0:T(8,128)S(1)}, f32[8,128,64]{1,2,0:T(8,128)S(1)}, u32[]{:S(2)}, u32[]{:S(2)}) collective-permute-start(f32[8,128,64]{1,2,0:T(8,128)S(1)} %add.158), channel_id=1, source_target_pairs={{0,2},{1,3},{2,0},{3,1},{4,6},{5,7},{6,4},{7,5},{8,10},{9,11},{10,... | collective-permute-start | bytes 786440 | tf_op jit(solution)/shard_map/ppermute | solution.py:42
  170.6 148.4 %all-reduce.14.cloned.1.call-start = ((), (), s32[]{:S(2)}) async-start(), calls=%async_computation.2 | async-start | bytes 2097152 | tf_op jit(solution)/shard_map/psum | solution.py:68
  224.2 14.7 %copy-start.2 = (bf16[8,16,128,128]{3,2,1,0:T(8,128)(2,1)S(1)}, bf16[8,16,128,128]{3,2,1,0:T(8,128)(2,1)}, u32[]{:S(2)}) copy-start(bf16[8,16,128,128]{3,2,1,0:T(8,128)(2,1)} %param.6) | copy-start | bytes 12582916
  228.7 1.6 collective-permute-start.4
  230.4 8.4 %collective-permute-start.5 = (f32[8,128,64]{1,2,0:T(8,128)S(1)}, f32[8,128,64]{1,2,0:T(8,128)S(1)}, u32[]{:S(2)}, u32[]{:S(2)}) collective-permute-start(f32[8,128,64]{1,2,0:T(8,128)S(1)} %add.162), channel_id=1, source_target_pairs={{0,2},{1,3},{2,0},{3,1},{4,6},{5,7},{6,4},{7,5},{8,10},{9,11},{10,... | collective-permute-start | bytes 786440 | tf_op jit(solution)/shard_map/ppermute | solution.py:42
  261.2 57.8 %copy-start.5 = (f32[4096,64]{0,1:T(8,128)S(1)}, f32[4096,64]{0,1:T(8,128)}, u32[]{:S(2)}) copy-start(f32[4096,64]{0,1:T(8,128)} %all-reduce.12.cloned.1.call-done) | copy-start | bytes 3145732
  267.6 167.0 %all-reduce.16.cloned.1.call-start = ((), (), s32[]{:S(2)}) async-start(), calls=%async_computation.3 | async-start | bytes 2097152 | tf_op jit(solution)/shard_map/psum | solution.py:68
  326.9 1.6 collective-permute-start.6
  328.6 8.4 %collective-permute-start.7 = (f32[8,128,64]{1,2,0:T(8,128)S(1)}, f32[8,128,64]{1,2,0:T(8,128)S(1)}, u32[]{:S(2)}, u32[]{:S(2)}) collective-permute-start(f32[8,128,64]{1,2,0:T(8,128)S(1)} %add.167), channel_id=1, source_target_pairs={{0,2},{1,3},{2,0},{3,1},{4,6},{5,7},{6,4},{7,5},{8,10},{9,11},{10,... | collective-permute-start | bytes 786440 | tf_op jit(solution)/shard_map/ppermute | solution.py:42
  384.6 146.2 %all-reduce.18.cloned.1.call-start = ((), (), s32[]{:S(2)}) async-start(), calls=%async_computation.4 | async-start | bytes 2097152 | tf_op jit(solution)/shard_map/psum | solution.py:68
  438.3 14.5 %copy-start.3 = (bf16[8,16,128,128]{3,2,1,0:T(8,128)(2,1)S(1)}, bf16[8,16,128,128]{3,2,1,0:T(8,128)(2,1)}, u32[]{:S(2)}) copy-start(bf16[8,16,128,128]{3,2,1,0:T(8,128)(2,1)} %param.6) | copy-start | bytes 12582916
  442.1 1.7 collective-permute-start.8
  443.8 8.7 %collective-permute-start.9 = (f32[8,128,64]{1,2,0:T(8,128)S(1)}, f32[8,128,64]{1,2,0:T(8,128)S(1)}, u32[]{:S(2)}, u32[]{:S(2)}) collective-permute-start(f32[8,128,64]{1,2,0:T(8,128)S(1)} %add.172), channel_id=1, source_target_pairs={{0,2},{1,3},{2,0},{3,1},{4,6},{5,7},{6,4},{7,5},{8,10},{9,11},{10,... | collective-permute-start | bytes 786440 | tf_op jit(solution)/shard_map/ppermute | solution.py:42
  474.0 56.8 %copy-start.6 = (f32[4096,64]{0,1:T(8,128)S(1)}, f32[4096,64]{0,1:T(8,128)}, u32[]{:S(2)}) copy-start(f32[4096,64]{0,1:T(8,128)} %get-tuple-element.33) | copy-start | bytes 3145732
  479.4 163.5 %all-reduce.20.cloned.1.call-start = ((), (), s32[]{:S(2)}) async-start(), calls=%async_computation.5 | async-start | bytes 2097152 | tf_op jit(solution)/shard_map/psum | solution.py:68
  536.9 1.6 collective-permute-start.10
  538.5 8.4 %collective-permute-start.11 = (f32[8,128,64]{1,2,0:T(8,128)S(1)}, f32[8,128,64]{1,2,0:T(8,128)S(1)}, u32[]{:S(2)}, u32[]{:S(2)}) collective-permute-start(f32[8,128,64]{1,2,0:T(8,128)S(1)} %add.177), channel_id=1, source_target_pairs={{0,2},{1,3},{2,0},{3,1},{4,6},{5,7},{6,4},{7,5},{8,10},{9,11},{10,... | collective-permute-start | bytes 786440 | tf_op jit(solution)/shard_map/ppermute | solution.py:42
  587.5 55.5 %copy-start.7 = (f32[4096,64]{0,1:T(8,128)S(1)}, f32[4096,64]{0,1:T(8,128)}, u32[]{:S(2)}) copy-start(f32[4096,64]{0,1:T(8,128)} %get-tuple-element.33) | copy-start | bytes 3145732
  644.3 15.5 %copy-start.1 = (s32[4096]{0:T(1024)S(1)}, s32[4096]{0:T(1024)}, u32[]{:S(2)}) copy-start(s32[4096]{0:T(1024)} %param.8) | copy-start | bytes 49156
  649.0 1.6 collective-permute-start.12
  650.7 8.4 %collective-permute-start.13 = (f32[8,128,64]{1,2,0:T(8,128)S(1)}, f32[8,128,64]{1,2,0:T(8,128)S(1)}, u32[]{:S(2)}, u32[]{:S(2)}) collective-permute-start(f32[8,128,64]{1,2,0:T(8,128)S(1)} %add.180), channel_id=1, source_target_pairs={{0,2},{1,3},{2,0},{3,1},{4,6},{5,7},{6,4},{7,5},{8,10},{9,11},{10,... | collective-permute-start | bytes 786440 | tf_op jit(solution)/shard_map/ppermute | solution.py:42
Sparse Core Ops, SparseCore 0:
  54.6 53.3 all-reduce.9
  170.7 49.9 all-reduce.11
  267.8 51.1 all-reduce.13
  384.7 49.9 all-reduce.15
  479.6 51.1 all-reduce.17
  593.0 49.9 all-reduce.19
